TPU v7x, 128 devices: a whole 4x4x4 slice. The times are simulated.
128 devices in a mesh: grp: 8 (over z, core), narrow: 16 (over y, x).
Axes of the slice: x: 4, y: 4, z: 4, core: 2. Of those that a mesh axis runs over, the one named last changes fastest.
Arguments:
- panel: bfloat16 [64, 229376], P(None, ('grp', 'narrow')), may hold values from -6 to 6
- tiles: bfloat16 [65536, 128, 128], P(('grp', 'narrow')), may hold values from -0.125 to 0.125
- tile_row: int32 [65536], P(('grp', 'narrow')), may hold values from 0 to 1791, as said below
- tile_col: int32 [65536], P(('grp', 'narrow')), may hold values from 0 to 1791, as said below
- tile_count: int32 [128], P(('grp', 'narrow')), may hold values from 128 to 512, as said below
Outputs:
- filtered: bfloat16 [64, 229376], P(None, ('grp', 'narrow'))
- normal_image: float32 [64, 229376], P(None, ('grp', 'narrow'))
Inputs may be any that keep to these rules, and one draw needn't show every extreme that they name: tile_row of a slot on a device of grp index g lies in g * 224 .. (g + 1) * 224 - 1. tile_col of a slot on a device of grp index g lies in (g - 1) * 224 .. (g + 1) * 224 - 1, and in g * 224 .. for g = 0. `tile_count`: some device holds 512 live slots.
All inputs are finite; a program needn't handle non-finite values.
Results may differ from a plain program's by a relative error of at most 0.009.
Values may be sent and summed in bfloat16 or wider, within the bound.
No kernel may reach another device: no remote copies, remote signals or barrier semaphores. Data moves between devices by JAX's collectives and lax.ppermute only.
A program may use at most 128 MiB of HBM per device.

v0:
```python
import jax
import jax.numpy as jnp
from jax import lax
from jax.sharding import PartitionSpec as P


def shifted(value, axis, steps):
    count = lax.axis_size(axis)
    initial, last = (max(0, -steps), min(count, count - steps))
    return lax.ppermute(value, axis, [(source, source + steps) for source in range(initial, last)])


def body(panel, tiles, tile_row, tile_col, tile_count):
    cols = panel.shape[0]
    tile = tiles.shape[1]
    slots = tiles.shape[0]
    nbd = panel.shape[1] // tile
    nbg = nbd * lax.axis_size("narrow")
    group = lax.axis_index("grp")
    prior_piece = shifted(panel, "grp", 1)
    own_all, prior_all = (
        lax.all_gather(panel, "narrow", axis=1, tiled=True),
        lax.all_gather(prior_piece, "narrow", axis=1, tiled=True),
    )
    both = jnp.concatenate([prior_all, own_all], axis=1).reshape(cols, 2 * nbg, tile)
    local_row = tile_row - group * nbg
    local_col = tile_col - (group - 1) * nbg
    count = tile_count[0]
    block = min(64, slots)
    turns = (count + block - 1) // block

    def pick(start):
        part = lax.dynamic_slice_in_dim(tiles, start, block, 0)
        rowidx = lax.dynamic_slice_in_dim(local_row, start, block, 0)
        colidx = lax.dynamic_slice_in_dim(local_col, start, block, 0)
        live = (start + jnp.arange(block) < count).astype(jnp.float32)
        return (part, rowidx, colidx, live)

    def forward(step, acc):
        part, rowidx, colidx, live = pick(step * block)
        pieces = jnp.take(both, colidx, axis=1)
        prod = jnp.einsum("kti,tji->ktj", pieces, part, preferred_element_type=jnp.float32)
        return acc.at[:, rowidx, :].add(prod * live[None, :, None])

    ystart = jnp.zeros((cols, nbg, tile), jnp.float32)
    row_part = lax.fori_loop(0, turns, forward, ystart).reshape(cols, nbg * tile)
    mine = lax.psum_scatter(row_part, "narrow", scatter_dimension=1, tiled=True)
    filtered = mine.astype(jnp.bfloat16)
    group_rows = lax.all_gather(filtered, "narrow", axis=1, tiled=True)
    group_blocks = group_rows.reshape(cols, nbg, tile)

    def backward(step, acc):
        part, rowidx, colidx, live = pick(step * block)
        pieces = jnp.take(group_blocks, rowidx, axis=1)
        prod = jnp.einsum("ktj,tji->kti", pieces, part, preferred_element_type=jnp.float32)
        return acc.at[:, colidx, :].add(prod * live[None, :, None])

    zstart = jnp.zeros((cols, 2 * nbg, tile), jnp.float32)
    col_part = lax.fori_loop(0, turns, backward, zstart)
    prior_term = col_part[:, :nbg, :].reshape(cols, nbg * tile)
    own_term = col_part[:, nbg:, :].reshape(cols, nbg * tile)
    own_sum, prior_sum = (
        lax.psum_scatter(
            own_term.astype(jnp.bfloat16), "narrow", scatter_dimension=1, tiled=True
        ).astype(jnp.float32),
        lax.psum_scatter(
            prior_term.astype(jnp.bfloat16), "narrow", scatter_dimension=1, tiled=True
        ).astype(jnp.float32),
    )
    from_next = shifted(prior_sum.astype(jnp.bfloat16), "grp", -1).astype(prior_sum.dtype)
    result = own_sum + from_next
    return (filtered, result)


def solution(mesh):
    placed = (
        P(None, ("grp", "narrow")),
        P(("grp", "narrow"), None, None),
        P(("grp", "narrow")),
        P(("grp", "narrow")),
        P(("grp", "narrow")),
    )
    return jax.shard_map(
        body,
        mesh=mesh,
        in_specs=placed,
        out_specs=(P(None, ("grp", "narrow")), P(None, ("grp", "narrow"))),
        check_vma=False,
    )
```

profile of v0, /device:TPU:0, one launch (start us, length us, event | category | flops | bytes accessed | tf_op | source)
XLA Modules:
  0.0 717.0 jit_solution(3994924240693866123)
XLA Ops:
  12.7 49.5 %all-gather.6.cloned.1.call-done = bf16[64,28672]{1,0:T(8,128)(2,1)} async-done(((bf16[64,1792]{1,0:T(8,128)(2,1)}), bf16[64,28672]{1,0:T(8,128)(2,1)}) %all-gather.6.cloned.1.call-update) | async-done | bytes 3670032 | tf_op jit(solution)/shard_map/all_gather | solution.py:22
  62.2 51.4 %all-gather.4.cloned.1.call-done = bf16[64,28672]{1,0:T(8,128)(2,1)} async-done(((bf16[64,1792]{1,0:T(8,128)(2,1)}), bf16[64,28672]{1,0:T(8,128)(2,1)}) %all-gather.4.cloned.1.call-update) | async-done | bytes 3670032 | tf_op jit(solution)/shard_map/all_gather | solution.py:23
  124.5 135.5 %while.20 = (s32[]{:T(128)}, f32[64,224,128]{2,0,1:T(8,128)}, s32[]{:T(128)}, s32[512]{0:T(512)S(1)}, bf16[512,128,128]{2,1,0:T(8,128)(2,1)}, /*index=5*/s32[512...) while((s32[]{:T(128)}, f32[64,224,128]{2,0,1:T(8,128)}, ...), condition=%wide.region_2.3_spmd, body=%wide.region_0.2_spmd.sunk | while | flops 135792384 | bytes 13638199 | solution.py:46
  132.2 9.1 %scatter_fusion = f32[64,224,128]{2,0,1:T(8,128)} fusion(f32[64,224,128]{2,0,1:T(8,128)} %get-tuple-element.281, s32[64]{0:T(128)S(1)} %compare_select_fusion.8, f32[64,64,128]{2,1,0:T(8,128)S(1)} %multiply_bitcast_fusion.4), kind=kCustom, calls=%fused_computation.2.clone.1 | custom fusion | flops 524288 | bytes 6291712 | tf_op jit(solution)/shard_map/while/body/scatter-add | solution.py:43
  149.1 9.2 %scatter_fusion = f32[64,224,128]{2,0,1:T(8,128)} fusion(f32[64,224,128]{2,0,1:T(8,128)} %get-tuple-element.281, s32[64]{0:T(128)S(1)} %compare_select_fusion.8, f32[64,64,128]{2,1,0:T(8,128)S(1)} %multiply_bitcast_fusion.4), kind=kCustom, calls=%fused_computation.2.clone.1 | custom fusion | flops 524288 | bytes 6291712 | tf_op jit(solution)/shard_map/while/body/scatter-add | solution.py:43
  166.1 9.1 %scatter_fusion = f32[64,224,128]{2,0,1:T(8,128)} fusion(f32[64,224,128]{2,0,1:T(8,128)} %get-tuple-element.281, s32[64]{0:T(128)S(1)} %compare_select_fusion.8, f32[64,64,128]{2,1,0:T(8,128)S(1)} %multiply_bitcast_fusion.4), kind=kCustom, calls=%fused_computation.2.clone.1 | custom fusion | flops 524288 | bytes 6291712 | tf_op jit(solution)/shard_map/while/body/scatter-add | solution.py:43
  183.0 9.2 %scatter_fusion = f32[64,224,128]{2,0,1:T(8,128)} fusion(f32[64,224,128]{2,0,1:T(8,128)} %get-tuple-element.281, s32[64]{0:T(128)S(1)} %compare_select_fusion.8, f32[64,64,128]{2,1,0:T(8,128)S(1)} %multiply_bitcast_fusion.4), kind=kCustom, calls=%fused_computation.2.clone.1 | custom fusion | flops 524288 | bytes 6291712 | tf_op jit(solution)/shard_map/while/body/scatter-add | solution.py:43
  199.9 9.2 %scatter_fusion = f32[64,224,128]{2,0,1:T(8,128)} fusion(f32[64,224,128]{2,0,1:T(8,128)} %get-tuple-element.281, s32[64]{0:T(128)S(1)} %compare_select_fusion.8, f32[64,64,128]{2,1,0:T(8,128)S(1)} %multiply_bitcast_fusion.4), kind=kCustom, calls=%fused_computation.2.clone.1 | custom fusion | flops 524288 | bytes 6291712 | tf_op jit(solution)/shard_map/while/body/scatter-add | solution.py:43
  216.9 9.1 %scatter_fusion = f32[64,224,128]{2,0,1:T(8,128)} fusion(f32[64,224,128]{2,0,1:T(8,128)} %get-tuple-element.281, s32[64]{0:T(128)S(1)} %compare_select_fusion.8, f32[64,64,128]{2,1,0:T(8,128)S(1)} %multiply_bitcast_fusion.4), kind=kCustom, calls=%fused_computation.2.clone.1 | custom fusion | flops 524288 | bytes 6291712 | tf_op jit(solution)/shard_map/while/body/scatter-add | solution.py:43
  233.9 9.1 %scatter_fusion = f32[64,224,128]{2,0,1:T(8,128)} fusion(f32[64,224,128]{2,0,1:T(8,128)} %get-tuple-element.281, s32[64]{0:T(128)S(1)} %compare_select_fusion.8, f32[64,64,128]{2,1,0:T(8,128)S(1)} %multiply_bitcast_fusion.4), kind=kCustom, calls=%fused_computation.2.clone.1 | custom fusion | flops 524288 | bytes 6291712 | tf_op jit(solution)/shard_map/while/body/scatter-add | solution.py:43
  250.8 9.2 %scatter_fusion = f32[64,224,128]{2,0,1:T(8,128)} fusion(f32[64,224,128]{2,0,1:T(8,128)} %get-tuple-element.281, s32[64]{0:T(128)S(1)} %compare_select_fusion.8, f32[64,64,128]{2,1,0:T(8,128)S(1)} %multiply_bitcast_fusion.4), kind=kCustom, calls=%fused_computation.2.clone.1 | custom fusion | flops 524288 | bytes 6291712 | tf_op jit(solution)/shard_map/while/body/scatter-add | solution.py:43
  266.5 82.3 %reduce-scatter.4.cloned.1.call-done = f32[64,1792]{1,0:T(8,128)} async-done(((f32[64,28672]{1,0:T(8,128)}), f32[64,1792]{1,0:T(8,128)}) %reduce-scatter.4.cloned.1.call-update) | async-done | bytes 458768 | tf_op jit(solution)/shard_map/reduce_scatter | solution.py:47
  350.6 49.8 %all-gather.8.cloned.1.call-done = bf16[64,28672]{1,0:T(8,128)(2,1)} async-done(((bf16[64,1792]{1,0:T(8,128)(2,1)}), bf16[64,28672]{1,0:T(8,128)(2,1)}) %all-gather.8.cloned.1.call-update) | async-done | bytes 3670032 | tf_op jit(solution)/shard_map/all_gather | solution.py:49
  412.4 120.7 %while.21 = (s32[]{:T(128)}, f32[64,448,128]{2,0,1:T(8,128)}, s32[]{:T(128)}, s32[512]{0:T(512)S(1)}, bf16[512,128,128]{2,1,0:T(8,128)(2,1)}, /*index=5*/s32[512...) while((s32[]{:T(128)}, f32[64,448,128]{2,0,1:T(8,128)}, ...), condition=%wide.region_6.7_spmd, body=%wide.region_4.6_spmd.sunk | while | flops 135792384 | bytes 13638199 | solution.py:59
  418.3 9.1 %scatter_fusion.1 = f32[64,448,128]{2,0,1:T(8,128)} fusion(f32[64,448,128]{2,0,1:T(8,128)} %get-tuple-element.317, s32[64]{0:T(128)S(1)} %compare_select_fusion.9, f32[64,64,128]{2,1,0:T(8,128)S(1)} %multiply_bitcast_fusion.5), kind=kCustom, calls=%fused_computation.3.clone.1 | custom fusion | flops 524288 | bytes 6291712 | tf_op jit(solution)/shard_map/while/body/scatter-add | solution.py:56
  433.4 9.2 %scatter_fusion.1 = f32[64,448,128]{2,0,1:T(8,128)} fusion(f32[64,448,128]{2,0,1:T(8,128)} %get-tuple-element.317, s32[64]{0:T(128)S(1)} %compare_select_fusion.9, f32[64,64,128]{2,1,0:T(8,128)S(1)} %multiply_bitcast_fusion.5), kind=kCustom, calls=%fused_computation.3.clone.1 | custom fusion | flops 524288 | bytes 6291712 | tf_op jit(solution)/shard_map/while/body/scatter-add | solution.py:56
  448.6 9.2 %scatter_fusion.1 = f32[64,448,128]{2,0,1:T(8,128)} fusion(f32[64,448,128]{2,0,1:T(8,128)} %get-tuple-element.317, s32[64]{0:T(128)S(1)} %compare_select_fusion.9, f32[64,64,128]{2,1,0:T(8,128)S(1)} %multiply_bitcast_fusion.5), kind=kCustom, calls=%fused_computation.3.clone.1 | custom fusion | flops 524288 | bytes 6291712 | tf_op jit(solution)/shard_map/while/body/scatter-add | solution.py:56
  463.7 9.2 %scatter_fusion.1 = f32[64,448,128]{2,0,1:T(8,128)} fusion(f32[64,448,128]{2,0,1:T(8,128)} %get-tuple-element.317, s32[64]{0:T(128)S(1)} %compare_select_fusion.9, f32[64,64,128]{2,1,0:T(8,128)S(1)} %multiply_bitcast_fusion.5), kind=kCustom, calls=%fused_computation.3.clone.1 | custom fusion | flops 524288 | bytes 6291712 | tf_op jit(solution)/shard_map/while/body/scatter-add | solution.py:56
  478.8 9.1 %scatter_fusion.1 = f32[64,448,128]{2,0,1:T(8,128)} fusion(f32[64,448,128]{2,0,1:T(8,128)} %get-tuple-element.317, s32[64]{0:T(128)S(1)} %compare_select_fusion.9, f32[64,64,128]{2,1,0:T(8,128)S(1)} %multiply_bitcast_fusion.5), kind=kCustom, calls=%fused_computation.3.clone.1 | custom fusion | flops 524288 | bytes 6291712 | tf_op jit(solution)/shard_map/while/body/scatter-add | solution.py:56
  493.8 9.2 %scatter_fusion.1 = f32[64,448,128]{2,0,1:T(8,128)} fusion(f32[64,448,128]{2,0,1:T(8,128)} %get-tuple-element.317, s32[64]{0:T(128)S(1)} %compare_select_fusion.9, f32[64,64,128]{2,1,0:T(8,128)S(1)} %multiply_bitcast_fusion.5), kind=kCustom, calls=%fused_computation.3.clone.1 | custom fusion | flops 524288 | bytes 6291712 | tf_op jit(solution)/shard_map/while/body/scatter-add | solution.py:56
  509.0 9.1 %scatter_fusion.1 = f32[64,448,128]{2,0,1:T(8,128)} fusion(f32[64,448,128]{2,0,1:T(8,128)} %get-tuple-element.317, s32[64]{0:T(128)S(1)} %compare_select_fusion.9, f32[64,64,128]{2,1,0:T(8,128)S(1)} %multiply_bitcast_fusion.5), kind=kCustom, calls=%fused_computation.3.clone.1 | custom fusion | flops 524288 | bytes 6291712 | tf_op jit(solution)/shard_map/while/body/scatter-add | solution.py:56
  533.1 10.1 %convert.4 = bf16[64,448,128]{2,0,1:T(8,128)(2,1)} convert(f32[64,448,128]{2,0,1:T(8,128)} %get-tuple-element.89) | non-fusion elementwise | flops 3670016 | bytes 22020096 | tf_op jit(solution)/shard_map/convert.1
  557.2 71.5 %reduce-scatter.8.cloned.1.call-done = bf16[64,1792]{1,0:T(8,128)(2,1)} async-done(((bf16[64,28672]{1,0:T(8,128)(2,1)}), bf16[64,1792]{1,0:T(8,128)(2,1)}) %reduce-scatter.8.cloned.1.call-update) | async-done | bytes 229392 | tf_op jit(solution)/shard_map/reduce_scatter | solution.py:66
  629.9 78.5 %reduce-scatter.6.cloned.1.call-done = bf16[64,1792]{1,0:T(8,128)(2,1)} async-done(((bf16[64,28672]{1,0:T(8,128)(2,1)}), bf16[64,1792]{1,0:T(8,128)(2,1)}) %reduce-scatter.6.cloned.1.call-update) | async-done | bytes 229392 | tf_op jit(solution)/shard_map/reduce_scatter | solution.py:63
  (110 shorter events, 171.5 us)
Async XLA Ops:
  7.2 55.1 %all-gather.6.cloned.1.call-start = ((), (), s32[]{:S(2)}) async-start(), calls=%async_computation.4 | async-start | bytes 3899392 | tf_op jit(solution)/shard_map/all_gather | solution.py:22
  7.9 105.7 %all-gather.4.cloned.1.call-start = ((), (), s32[]{:S(2)}) async-start(), calls=%async_computation.3 | async-start | bytes 3899392 | tf_op jit(solution)/shard_map/all_gather | solution.py:23
  7.9 2.6 collective-permute-start
  10.5 0.7 copy-start
  11.3 337.5 %reduce-scatter.4.cloned.1.call-start = ((), (), s32[]{:S(2)}) async-start(), calls=%async_computation.5 | async-start | bytes 7798784 | tf_op jit(solution)/shard_map/reduce_scatter | solution.py:47
  266.5 133.9 %all-gather.8.cloned.1.call-start = ((), (), s32[]{:S(2)}) async-start(), calls=%async_computation.6 | async-start | bytes 3899392 | tf_op jit(solution)/shard_map/all_gather | solution.py:49
  350.6 278.1 %reduce-scatter.8.cloned.1.call-start = ((), (), s32[]{:S(2)}) async-start(), calls=%async_computation.8 | async-start | bytes 3899392 | tf_op jit(solution)/shard_map/reduce_scatter | solution.py:66
  552.5 155.9 %reduce-scatter.6.cloned.1.call-start = ((), (), s32[]{:S(2)}) async-start(), calls=%async_computation.7 | async-start | bytes 3899392 | tf_op jit(solution)/shard_map/reduce_scatter | solution.py:63
  628.6 79.8 %collective-permute-start.1 = (bf16[64,1792]{1,0:T(8,128)(2,1)}, bf16[64,1792]{1,0:T(8,128)(2,1)S(1)}, u32[]{:S(2)}, u32[]{:S(2)}) collective-permute-start(bf16[64,1792]{1,0:T(8,128)(2,1)} %reduce-scatter.8.cloned.1.call-done), channel_id=1, source_target_pairs={{16,0},{32,16},{48,32},{64,48},{80,64},{96,80},{112,96},{17,1},{33... | collective-permute-start | bytes 688136 | tf_op jit(solution)/shard_map/ppermute | solution.py:10
Sparse Core Ops, SparseCore 0:
  10.2 52.0 all-gather.5
  65.0 48.5 all-gather.3
  266.6 82.1 reduce-scatter.3
  351.4 48.9 all-gather.7
  552.6 75.9 reduce-scatter.7
  631.9 76.4 reduce-scatter.5
where the time goes:
time: 724 us; the launch traced here: 717 us
  waiting for transfers between devices  385 us (53%)
  other arithmetic  180 us (25%)
  local copies, waits for them, and re-layouts  89.9 us (12%)
  matrix products  43.7 us (6%)
  between operations  14.8 us (2%)
    reduce_scatter x1, waiting for transfers between devices, body(): mine = lax.psum_scatter(row_part, 'narrow', scatter_dimension=1, tiled=True)  82.3 us
    reduce_scatter x1, waiting for transfers between devices, body(): lax.psum_scatter(own_term.astype(jnp.bfloat16), 'narrow', scatter_dimensi...  78.5 us
    scatter-add x8, other arithmetic, backward(): return acc.at[:, colidx, :].add(prod * live[None, :, None])  73.2 us
    scatter-add x8, other arithmetic, forward(): return acc.at[:, rowidx, :].add(prod * live[None, :, None])  73.2 us
    reduce_scatter x1, waiting for transfers between devices, body(): lax.psum_scatter(prior_term.astype(jnp.bfloat16), 'narrow', scatter_dimen...  71.5 us
    all_gather x1, waiting for transfers between devices, body(): lax.all_gather(prior_piece, 'narrow', axis=1, tiled=True)  51.4 us
    all_gather x1, waiting for transfers between devices, body(): group_rows = lax.all_gather(filtered, 'narrow', axis=1, tiled=True)  49.8 us
    all_gather x1, waiting for transfers between devices, body(): lax.all_gather(panel, 'narrow', axis=1, tiled=True)  49.5 us
  transfers between devices with their start and end apart: 8, of which 7 were waited for; matrix products, arithmetic and copies ran while one was open for 1% of the time, Pallas kernels for 0%

commit v1 on v0

--- a/solution.py
+++ b/solution.py
@@ -2,6 +2,11 @@
 import jax.numpy as jnp
 from jax import lax
 from jax.sharding import PartitionSpec as P
+
+
+def gather_over(array, name, dim):
+    stack = jnp.stack([array] * lax.axis_size(name))
+    return jnp.concatenate(lax.all_to_all(stack, name, 0, 0), axis=dim)
 
 
 def shifted(value, axis, steps):
@@ -46,7 +51,7 @@
     row_part = lax.fori_loop(0, turns, forward, ystart).reshape(cols, nbg * tile)
     mine = lax.psum_scatter(row_part, "narrow", scatter_dimension=1, tiled=True)
     filtered = mine.astype(jnp.bfloat16)
-    group_rows = lax.all_gather(filtered, "narrow", axis=1, tiled=True)
+    group_rows = gather_over(filtered, "narrow", 1)
     group_blocks = group_rows.reshape(cols, nbg, tile)
 
     def backward(step, acc):

time: 724 us -> 747 us (1.032)
  local copies, waits for them, and re-layouts: 89.9 us -> 106 us
    all_to_all x0 -> x1, waiting for transfers between devices: none -> 52.1 us  [gather_over(): return jnp.concatenate(lax.all_to_all(stack, name, 0, 0), axis=dim)]
    all_gather x1 -> x0, waiting for transfers between devices: 49.8 us -> none  [body(): group_rows = lax.all_gather(filtered, 'narrow', axis=1, tiled=True)]
    another operation x0 -> x2, local copies, waits for them, and re-layouts: none -> 10.2 us  [the longest x1 8.03 us: body(): group_blocks = group_rows.reshape(cols, nbg, tile)]
where the time goes in v1:
time: 747 us; the launch traced here: 739 us
  waiting for transfers between devices  387 us (52%)
  other arithmetic  180 us (24%)
  local copies, waits for them, and re-layouts  106 us (14%)
  matrix products  43.7 us (6%)
  between operations  14.5 us (2%)
  starting transfers between devices  7.77 us (1%)
    reduce_scatter x1, waiting for transfers between devices, body(): mine = lax.psum_scatter(row_part, 'narrow', scatter_dimension=1, tiled=True)  82.4 us
    reduce_scatter x1, waiting for transfers between devices, body(): lax.psum_scatter(own_term.astype(jnp.bfloat16), 'narrow', scatter_dimensi...  78.5 us
    scatter-add x8, other arithmetic, backward(): return acc.at[:, colidx, :].add(prod * live[None, :, None])  73.2 us
    scatter-add x8, other arithmetic, forward(): return acc.at[:, rowidx, :].add(prod * live[None, :, None])  73.2 us
    reduce_scatter x1, waiting for transfers between devices, body(): lax.psum_scatter(prior_term.astype(jnp.bfloat16), 'narrow', scatter_dimen...  70.6 us
    all_to_all x1, waiting for transfers between devices, gather_over(): return jnp.concatenate(lax.all_to_all(stack, name, 0, 0), axis=dim)  52.1 us
    all_gather x1, waiting for transfers between devices, body(): lax.all_gather(prior_piece, 'narrow', axis=1, tiled=True)  51.4 us
    all_gather x1, waiting for transfers between devices, body(): lax.all_gather(panel, 'narrow', axis=1, tiled=True)  49.5 us
  transfers between devices with their start and end apart: 8, of which 7 were waited for; matrix products, arithmetic and copies ran while one was open for 1% of the time, Pallas kernels for 0%

profile of v1, /device:TPU:0, one launch (start us, length us, event | category | flops | bytes accessed | tf_op | source)
XLA Modules:
  0.0 739.0 jit_solution(8874654010258004688)
XLA Ops:
  12.7 49.5 %all-gather.5.cloned.1.call-done = bf16[64,28672]{1,0:T(8,128)(2,1)} async-done(((bf16[64,1792]{1,0:T(8,128)(2,1)}), bf16[64,28672]{1,0:T(8,128)(2,1)}) %all-gather.5.cloned.1.call-update) | async-done | bytes 3670032 | tf_op jit(solution)/shard_map/all_gather | solution.py:27
  62.2 51.4 %all-gather.3.cloned.1.call-done = bf16[64,28672]{1,0:T(8,128)(2,1)} async-done(((bf16[64,1792]{1,0:T(8,128)(2,1)}), bf16[64,28672]{1,0:T(8,128)(2,1)}) %all-gather.3.cloned.1.call-update) | async-done | bytes 3670032 | tf_op jit(solution)/shard_map/all_gather | solution.py:28
  124.5 135.5 %while.20 = (s32[]{:T(128)}, f32[64,224,128]{2,0,1:T(8,128)}, s32[]{:T(128)}, s32[512]{0:T(512)S(1)}, bf16[512,128,128]{2,1,0:T(8,128)(2,1)}, /*index=5*/s32[512...) while((s32[]{:T(128)}, f32[64,224,128]{2,0,1:T(8,128)}, ...), condition=%wide.region_2.3_spmd, body=%wide.region_0.2_spmd.sunk | while | flops 135792384 | bytes 13638199 | solution.py:51
  132.2 9.1 %scatter_fusion = f32[64,224,128]{2,0,1:T(8,128)} fusion(f32[64,224,128]{2,0,1:T(8,128)} %get-tuple-element.289, s32[64]{0:T(128)S(1)} %compare_select_fusion.8, f32[64,64,128]{2,1,0:T(8,128)S(1)} %multiply_bitcast_fusion.4), kind=kCustom, calls=%fused_computation.2.clone.1 | custom fusion | flops 524288 | bytes 6291712 | tf_op jit(solution)/shard_map/while/body/scatter-add | solution.py:48
  149.1 9.2 %scatter_fusion = f32[64,224,128]{2,0,1:T(8,128)} fusion(f32[64,224,128]{2,0,1:T(8,128)} %get-tuple-element.289, s32[64]{0:T(128)S(1)} %compare_select_fusion.8, f32[64,64,128]{2,1,0:T(8,128)S(1)} %multiply_bitcast_fusion.4), kind=kCustom, calls=%fused_computation.2.clone.1 | custom fusion | flops 524288 | bytes 6291712 | tf_op jit(solution)/shard_map/while/body/scatter-add | solution.py:48
  166.1 9.1 %scatter_fusion = f32[64,224,128]{2,0,1:T(8,128)} fusion(f32[64,224,128]{2,0,1:T(8,128)} %get-tuple-element.289, s32[64]{0:T(128)S(1)} %compare_select_fusion.8, f32[64,64,128]{2,1,0:T(8,128)S(1)} %multiply_bitcast_fusion.4), kind=kCustom, calls=%fused_computation.2.clone.1 | custom fusion | flops 524288 | bytes 6291712 | tf_op jit(solution)/shard_map/while/body/scatter-add | solution.py:48
  183.0 9.2 %scatter_fusion = f32[64,224,128]{2,0,1:T(8,128)} fusion(f32[64,224,128]{2,0,1:T(8,128)} %get-tuple-element.289, s32[64]{0:T(128)S(1)} %compare_select_fusion.8, f32[64,64,128]{2,1,0:T(8,128)S(1)} %multiply_bitcast_fusion.4), kind=kCustom, calls=%fused_computation.2.clone.1 | custom fusion | flops 524288 | bytes 6291712 | tf_op jit(solution)/shard_map/while/body/scatter-add | solution.py:48
  199.9 9.2 %scatter_fusion = f32[64,224,128]{2,0,1:T(8,128)} fusion(f32[64,224,128]{2,0,1:T(8,128)} %get-tuple-element.289, s32[64]{0:T(128)S(1)} %compare_select_fusion.8, f32[64,64,128]{2,1,0:T(8,128)S(1)} %multiply_bitcast_fusion.4), kind=kCustom, calls=%fused_computation.2.clone.1 | custom fusion | flops 524288 | bytes 6291712 | tf_op jit(solution)/shard_map/while/body/scatter-add | solution.py:48
  216.9 9.1 %scatter_fusion = f32[64,224,128]{2,0,1:T(8,128)} fusion(f32[64,224,128]{2,0,1:T(8,128)} %get-tuple-element.289, s32[64]{0:T(128)S(1)} %compare_select_fusion.8, f32[64,64,128]{2,1,0:T(8,128)S(1)} %multiply_bitcast_fusion.4), kind=kCustom, calls=%fused_computation.2.clone.1 | custom fusion | flops 524288 | bytes 6291712 | tf_op jit(solution)/shard_map/while/body/scatter-add | solution.py:48
  233.8 9.1 %scatter_fusion = f32[64,224,128]{2,0,1:T(8,128)} fusion(f32[64,224,128]{2,0,1:T(8,128)} %get-tuple-element.289, s32[64]{0:T(128)S(1)} %compare_select_fusion.8, f32[64,64,128]{2,1,0:T(8,128)S(1)} %multiply_bitcast_fusion.4), kind=kCustom, calls=%fused_computation.2.clone.1 | custom fusion | flops 524288 | bytes 6291712 | tf_op jit(solution)/shard_map/while/body/scatter-add | solution.py:48
  250.8 9.2 %scatter_fusion = f32[64,224,128]{2,0,1:T(8,128)} fusion(f32[64,224,128]{2,0,1:T(8,128)} %get-tuple-element.289, s32[64]{0:T(128)S(1)} %compare_select_fusion.8, f32[64,64,128]{2,1,0:T(8,128)S(1)} %multiply_bitcast_fusion.4), kind=kCustom, calls=%fused_computation.2.clone.1 | custom fusion | flops 524288 | bytes 6291712 | tf_op jit(solution)/shard_map/while/body/scatter-add | solution.py:48
  266.5 82.4 %reduce-scatter.4.cloned.1.call-done = f32[64,1792]{1,0:T(8,128)} async-done(((f32[64,28672]{1,0:T(8,128)}), f32[64,1792]{1,0:T(8,128)}) %reduce-scatter.4.cloned.1.call-update) | async-done | bytes 458768 | tf_op jit(solution)/shard_map/reduce_scatter | solution.py:52
  357.2 52.1 %all-to-all-done = bf16[16,64,1792]{2,1,0:T(8,128)(2,1)} async-done(((bf16[16,64,1792]{2,1,0:T(8,128)(2,1)}), bf16[16,64,1792]{2,1,0:T(8,128)(2,1)}, u32[]{:S(2)}, u32[]{:S(2)}) %all-to-all-start) | async-done | bytes 3670048 | tf_op jit(solution)/shard_map/all_to_all | solution.py:9
  435.6 120.7 %while.21 = (s32[]{:T(128)}, f32[64,448,128]{2,0,1:T(8,128)}, s32[]{:T(128)}, s32[512]{0:T(512)S(1)}, bf16[512,128,128]{2,1,0:T(8,128)(2,1)}, /*index=5*/s32[512...) while((s32[]{:T(128)}, f32[64,448,128]{2,0,1:T(8,128)}, ...), condition=%wide.region_6.7_spmd, body=%wide.region_4.6_spmd.sunk | while | flops 135792384 | bytes 13638199 | solution.py:64
  441.5 9.1 %scatter_fusion.1 = f32[64,448,128]{2,0,1:T(8,128)} fusion(f32[64,448,128]{2,0,1:T(8,128)} %get-tuple-element.325, s32[64]{0:T(128)S(1)} %compare_select_fusion.9, f32[64,64,128]{2,1,0:T(8,128)S(1)} %multiply_bitcast_fusion.5), kind=kCustom, calls=%fused_computation.3.clone.1 | custom fusion | flops 524288 | bytes 6291712 | tf_op jit(solution)/shard_map/while/body/scatter-add | solution.py:61
  456.6 9.2 %scatter_fusion.1 = f32[64,448,128]{2,0,1:T(8,128)} fusion(f32[64,448,128]{2,0,1:T(8,128)} %get-tuple-element.325, s32[64]{0:T(128)S(1)} %compare_select_fusion.9, f32[64,64,128]{2,1,0:T(8,128)S(1)} %multiply_bitcast_fusion.5), kind=kCustom, calls=%fused_computation.3.clone.1 | custom fusion | flops 524288 | bytes 6291712 | tf_op jit(solution)/shard_map/while/body/scatter-add | solution.py:61
  471.7 9.2 %scatter_fusion.1 = f32[64,448,128]{2,0,1:T(8,128)} fusion(f32[64,448,128]{2,0,1:T(8,128)} %get-tuple-element.325, s32[64]{0:T(128)S(1)} %compare_select_fusion.9, f32[64,64,128]{2,1,0:T(8,128)S(1)} %multiply_bitcast_fusion.5), kind=kCustom, calls=%fused_computation.3.clone.1 | custom fusion | flops 524288 | bytes 6291712 | tf_op jit(solution)/shard_map/while/body/scatter-add | solution.py:61
  486.8 9.2 %scatter_fusion.1 = f32[64,448,128]{2,0,1:T(8,128)} fusion(f32[64,448,128]{2,0,1:T(8,128)} %get-tuple-element.325, s32[64]{0:T(128)S(1)} %compare_select_fusion.9, f32[64,64,128]{2,1,0:T(8,128)S(1)} %multiply_bitcast_fusion.5), kind=kCustom, calls=%fused_computation.3.clone.1 | custom fusion | flops 524288 | bytes 6291712 | tf_op jit(solution)/shard_map/while/body/scatter-add | solution.py:61
  501.9 9.1 %scatter_fusion.1 = f32[64,448,128]{2,0,1:T(8,128)} fusion(f32[64,448,128]{2,0,1:T(8,128)} %get-tuple-element.325, s32[64]{0:T(128)S(1)} %compare_select_fusion.9, f32[64,64,128]{2,1,0:T(8,128)S(1)} %multiply_bitcast_fusion.5), kind=kCustom, calls=%fused_computation.3.clone.1 | custom fusion | flops 524288 | bytes 6291712 | tf_op jit(solution)/shard_map/while/body/scatter-add | solution.py:61
  517.0 9.2 %scatter_fusion.1 = f32[64,448,128]{2,0,1:T(8,128)} fusion(f32[64,448,128]{2,0,1:T(8,128)} %get-tuple-element.325, s32[64]{0:T(128)S(1)} %compare_select_fusion.9, f32[64,64,128]{2,1,0:T(8,128)S(1)} %multiply_bitcast_fusion.5), kind=kCustom, calls=%fused_computation.3.clone.1 | custom fusion | flops 524288 | bytes 6291712 | tf_op jit(solution)/shard_map/while/body/scatter-add | solution.py:61
  532.2 9.1 %scatter_fusion.1 = f32[64,448,128]{2,0,1:T(8,128)} fusion(f32[64,448,128]{2,0,1:T(8,128)} %get-tuple-element.325, s32[64]{0:T(128)S(1)} %compare_select_fusion.9, f32[64,64,128]{2,1,0:T(8,128)S(1)} %multiply_bitcast_fusion.5), kind=kCustom, calls=%fused_computation.3.clone.1 | custom fusion | flops 524288 | bytes 6291712 | tf_op jit(solution)/shard_map/while/body/scatter-add | solution.py:61
  556.3 10.1 %convert.4 = bf16[64,448,128]{2,0,1:T(8,128)(2,1)} convert(f32[64,448,128]{2,0,1:T(8,128)} %get-tuple-element.89) | non-fusion elementwise | flops 3670016 | bytes 22020096 | tf_op jit(solution)/shard_map/convert.1
  580.4 70.6 %reduce-scatter.8.cloned.1.call-done = bf16[64,1792]{1,0:T(8,128)(2,1)} async-done(((bf16[64,28672]{1,0:T(8,128)(2,1)}), bf16[64,1792]{1,0:T(8,128)(2,1)}) %reduce-scatter.8.cloned.1.call-update) | async-done | bytes 229392 | tf_op jit(solution)/shard_map/reduce_scatter | solution.py:71
  652.2 78.5 %reduce-scatter.6.cloned.1.call-done = bf16[64,1792]{1,0:T(8,128)(2,1)} async-done(((bf16[64,28672]{1,0:T(8,128)(2,1)}), bf16[64,1792]{1,0:T(8,128)(2,1)}) %reduce-scatter.6.cloned.1.call-update) | async-done | bytes 229392 | tf_op jit(solution)/shard_map/reduce_scatter | solution.py:68
  (114 shorter events, 192.3 us)
Async XLA Ops:
  7.2 55.1 %all-gather.5.cloned.1.call-start = ((), (), s32[]{:S(2)}) async-start(), calls=%async_computation.5 | async-start | bytes 3899392 | tf_op jit(solution)/shard_map/all_gather | solution.py:27
  7.9 105.7 %all-gather.3.cloned.1.call-start = ((), (), s32[]{:S(2)}) async-start(), calls=%async_computation.4 | async-start | bytes 3899392 | tf_op jit(solution)/shard_map/all_gather | solution.py:28
  7.9 2.6 collective-permute-start
  10.5 0.7 copy-start.1
  11.3 337.6 %reduce-scatter.4.cloned.1.call-start = ((), (), s32[]{:S(2)}) async-start(), calls=%async_computation.6 | async-start | bytes 7798784 | tf_op jit(solution)/shard_map/reduce_scatter | solution.py:52
  349.9 65.3 %copy-start = (bf16[64,1792]{1,0:T(8,128)(2,1)}, bf16[64,1792]{1,0:T(8,128)(2,1)S(1)}, u32[]{:S(2)}) copy-start(bf16[64,1792]{1,0:T(8,128)(2,1)S(1)} %convert_element_type.33) | copy-start | bytes 688132
  352.1 57.2 %all-to-all-start = ((bf16[16,64,1792]{2,1,0:T(8,128)(2,1)}), bf16[16,64,1792]{2,1,0:T(8,128)(2,1)}, u32[]{:S(2)}, u32[]{:S(2)}) async-start(bf16[16,64,1792]{2,1,0:T(8,128)(2,1)} %stack.2), calls=%async_computation.1 | async-start | bytes 7340032 | tf_op jit(solution)/shard_map/all_to_all | solution.py:9
  357.1 293.8 %reduce-scatter.8.cloned.1.call-start = ((), (), s32[]{:S(2)}) async-start(), calls=%async_computation.8 | async-start | bytes 3899392 | tf_op jit(solution)/shard_map/reduce_scatter | solution.py:71
  575.7 155.1 %reduce-scatter.6.cloned.1.call-start = ((), (), s32[]{:S(2)}) async-start(), calls=%async_computation.7 | async-start | bytes 3899392 | tf_op jit(solution)/shard_map/reduce_scatter | solution.py:68
  650.9 79.8 %collective-permute-start.1 = (bf16[64,1792]{1,0:T(8,128)(2,1)}, bf16[64,1792]{1,0:T(8,128)(2,1)S(1)}, u32[]{:S(2)}, u32[]{:S(2)}) collective-permute-start(bf16[64,1792]{1,0:T(8,128)(2,1)} %reduce-scatter.8.cloned.1.call-done), channel_id=1, source_target_pairs={{16,0},{32,16},{48,32},{64,48},{80,64},{96,80},{112,96},{17,1},{33... | collective-permute-start | bytes 688136 | tf_op jit(solution)/shard_map/ppermute | solution.py:15
Sparse Core Ops, SparseCore 0:
  10.2 52.0 all-gather.4
  65.0 48.5 all-gather.2
  266.6 82.2 reduce-scatter.3
  575.8 75.0 reduce-scatter.7
  654.1 76.5 reduce-scatter.5
